TPU v7x, 128 devices: a whole 4x4x4 slice. The times are simulated.
128 devices in a mesh: blk: 16 (over y, z), rep: 8 (over x, core).
Axes of the slice: x: 4, y: 4, z: 4, core: 2. Of those that a mesh axis runs over, the one named last changes fastest.
Arguments:
- dense: bfloat16 [131072, 1024], P(('blk', 'rep')), may hold values from -6 to 6
- labels: int32 [131072], P(('blk', 'rep')), may hold values 0 or 1
- tile_values: bfloat16 [16384, 64, 128], P(('blk', 'rep')), may hold values from -1.1953125 to 1.1953125
- tile_block: int32 [16384, 64], P(('blk', 'rep')), may hold values from 0 to 1023
- tile_example: int32 [16384, 64], P(('blk', 'rep')), may hold values from 0 to 1023
- tile_count: int32 [16384], P(('blk', 'rep')), may hold values from 16 to 64, as said below
- z_state: float32 [131072, 128], P(('blk', 'rep')), may hold values from -6 to 6
- n_state: float32 [131072, 128], P(('blk', 'rep')), may hold values from 0.01 to 4
- w_one: bfloat16 [1024, 512], replicated, may hold values from -0.1875 to 0.1875
- b_one: float32 [512], replicated, may hold values from -3 to 3
- w_two: bfloat16 [512, 256], replicated, may hold values from -0.25 to 0.25
- b_two: float32 [256], replicated, may hold values from -3 to 3
- head: bfloat16 [256], replicated, may hold values from -0.375 to 0.375
Outputs:
- probability: float32 [131072], P(('blk', 'rep'))
- z_new: float32 [131072, 128], P(('blk', 'rep'))
- n_new: float32 [131072, 128], P(('blk', 'rep'))
- grad_w_one: float32 [1024, 512], replicated
- grad_b_one: float32 [512], replicated
- grad_w_two: float32 [512, 256], replicated
- grad_b_two: float32 [256], replicated
- grad_head: float32 [256], replicated
Inputs may be any that keep to these rules, and one draw needn't show every extreme that they name: `tile_count`: slots at or beyond a list's count are padding; in every draw some owners receive 64 live slots from every device.
All inputs are finite; a program needn't handle non-finite values. No bound on the sum of `labels` on one device may be relied on, other than what follows from the above.
Results may differ from a plain program's by a relative error of at most 0.013.
Values may be sent and summed in bfloat16 or wider, within the bound.
A program may use at most 64 MiB of HBM per device.

v0:
```python
import jax
import jax.numpy as jnp
from jax import lax
from jax.sharding import PartitionSpec as P

alpha_rate = 0.5
beta_shift = 1.0
lasso_term = 0.5
ridge_term = 0.1


def wide_weight(z_state, n_state):
    shrunk = z_state - jnp.sign(z_state) * lasso_term
    denominator = (beta_shift + jnp.sqrt(n_state)) / alpha_rate + ridge_term
    return jnp.where(jnp.abs(z_state) > lasso_term, -shrunk / denominator, jnp.zeros_like(z_state))


def silu_slope(pre):
    gate = jax.nn.sigmoid(pre)
    return gate * (1.0 + pre * (1.0 - gate))


def per_device(
    dense,
    labels,
    tile_values,
    tile_block,
    tile_example,
    tile_count,
    z_state,
    n_state,
    w_one,
    b_one,
    w_two,
    b_two,
    head,
):
    owners, capacity, width = tile_values.shape
    slots = jnp.arange(capacity, dtype=jnp.int32)
    live = slots[None, :] < tile_count[:, None]
    masked = jnp.where(live[:, :, None], tile_values, jnp.zeros_like(tile_values))
    got_values, got_block = (
        lax.all_to_all(masked, ("blk", "rep"), split_axis=0, concat_axis=0, tiled=True),
        lax.all_to_all(tile_block, ("blk", "rep"), split_axis=0, concat_axis=0, tiled=True),
    )
    weight = wide_weight(z_state, n_state)
    flat_block = got_block.reshape(-1)
    flat_values = got_values.reshape(-1, width)
    picked = jnp.take(weight, flat_block, axis=0)
    tile_logit = jnp.sum(flat_values.astype(jnp.float32) * picked, axis=1).reshape(owners, capacity)
    returned = lax.all_to_all(tile_logit, ("blk", "rep"), split_axis=0, concat_axis=0, tiled=True)
    flat_example = tile_example.reshape(-1)
    wide = jnp.zeros((dense.shape[0],), jnp.float32).at[flat_example].add(returned.reshape(-1))
    pre_one = jnp.dot(dense, w_one, preferred_element_type=jnp.float32) + b_one
    hid_one = jax.nn.silu(pre_one).astype(jnp.bfloat16)
    pre_two = jnp.dot(hid_one, w_two, preferred_element_type=jnp.float32) + b_two
    hid_two = jax.nn.silu(pre_two).astype(jnp.bfloat16)
    deep = jnp.dot(hid_two, head, preferred_element_type=jnp.float32)
    probability = jax.nn.sigmoid(wide + deep)
    residual = probability - labels.astype(jnp.float32)
    tile_residual = jnp.take(residual, flat_example).reshape(owners, capacity)
    got_residual = lax.all_to_all(
        tile_residual, ("blk", "rep"), split_axis=0, concat_axis=0, tiled=True
    )
    contrib = flat_values.astype(jnp.float32) * got_residual.reshape(-1)[:, None]
    grad_block = jnp.zeros_like(z_state).at[flat_block].add(contrib)
    n_new = n_state + grad_block * grad_block
    sigma = (jnp.sqrt(n_new) - jnp.sqrt(n_state)) / alpha_rate
    z_new = z_state + grad_block - sigma * weight
    dlogit = residual.astype(jnp.bfloat16)
    grad_head = jnp.dot(dlogit, hid_two, preferred_element_type=jnp.float32)
    d_two = (
        dlogit.astype(jnp.float32)[:, None]
        * head.astype(jnp.float32)[None, :]
        * silu_slope(pre_two)
    ).astype(jnp.bfloat16)
    grad_w_two = lax.dot_general(
        hid_one, d_two, (((0,), (0,)), ((), ())), preferred_element_type=jnp.float32
    )
    grad_b_two = jnp.sum(d_two.astype(jnp.float32), axis=0)
    back_one = lax.dot_general(
        d_two, w_two, (((1,), (1,)), ((), ())), preferred_element_type=jnp.float32
    )
    d_one = (back_one * silu_slope(pre_one)).astype(jnp.bfloat16)
    grad_w_one = lax.dot_general(
        dense, d_one, (((0,), (0,)), ((), ())), preferred_element_type=jnp.float32
    )
    grad_b_one = jnp.sum(d_one.astype(jnp.float32), axis=0)
    grad_head, grad_w_two, grad_b_two, grad_w_one, grad_b_one = lax.psum(
        (grad_head, grad_w_two, grad_b_two, grad_w_one, grad_b_one), ("blk", "rep")
    )
    return (probability, z_new, n_new, grad_w_one, grad_b_one, grad_w_two, grad_b_two, grad_head)


def solution(mesh):
    placed = (
        P(("blk", "rep"), None),
        P(("blk", "rep")),
        P(("blk", "rep"), None, None),
        P(("blk", "rep"), None),
        P(("blk", "rep"), None),
        P(("blk", "rep")),
        P(("blk", "rep"), None),
        P(("blk", "rep"), None),
        P(),
        P(),
        P(),
        P(),
        P(),
    )
    return jax.shard_map(
        per_device,
        mesh=mesh,
        in_specs=placed,
        out_specs=(
            P(("blk", "rep")),
            P(("blk", "rep"), None),
            P(("blk", "rep"), None),
            P(),
            P(),
            P(),
            P(),
            P(),
        ),
        check_vma=False,
    )
```

profile of v0, /device:TPU:1, one launch (start us, length us, event | category | flops | bytes accessed | tf_op | source)
XLA Modules:
  0.0 373.5 jit_solution(6273867925865264041)
XLA Ops:
  7.2 1.6 copy.30
  8.8 11.5 %all-to-all-start.1 = ((s32[128,1,64]{2,1,0:T(1,128)}), s32[128,1,64]{2,1,0:T(1,128)S(1)}, u32[]{:S(2)}, u32[]{:S(2)}) async-start(s32[128,1,64]{2,1,0:T(1,128)} %bitcast.2), calls=%async_computation.1 | async-start | bytes 131072 | tf_op jit(solution)/shard_map/all_to_all | solution.py:44
  20.3 0.7 iota_compare_fusion
  21.1 0.7 reshape.183
  21.7 0.8 copy.29
  22.7 1.6 divide_select_fusion
  24.4 4.5 %broadcast_select_fusion = bf16[128,64,128]{2,1,0:T(8,128)(2,1)} fusion(bf16[128,64,128]{2,1,0:T(8,128)(2,1)} %param.15, pred[128,64]{1,0:T(8,128)(4,1)S(1)} %iota_compare_fusion), kind=kLoop, calls=%fused_computation.10 | loop fusion | flops 1048576 | bytes 4202496 | tf_op jit(solution)/shard_map/jit(_where)/select_n | solution.py:41
  29.0 2.8 multiply_convert_fusion.1
  31.7 1.4 multiply_convert_fusion.3
  33.4 10.2 %all-to-all-start = ((bf16[128,64,128]{2,1,0:T(8,128)(2,1)}), bf16[128,64,128]{2,1,0:T(8,128)(2,1)}, u32[]{:S(2)}, u32[]{:S(2)}) async-start(bf16[128,64,128]{2,1,0:T(8,128)(2,1)} %broadcast_select_fusion), calls=%async_computation | async-start | bytes 4194304 | tf_op jit(solution)/shard_map/all_to_all | solution.py:43
  44.1 0.8 reduce.10
  45.1 27.8 %gather_fusion = f32[8192,128]{1,0:T(8,128)} fusion(f32[1024,128]{1,0:T(8,128)S(1)} %divide_select_fusion, s32[8192]{0:T(1024)S(1)} %broadcast_clamp_fusion.1), kind=kCustom, calls=%fused_computation | custom fusion | bytes 8421376 | tf_op jit(solution)/shard_map/jit(_take)/gather | solution.py:49
  72.9 0.9 all-to-all-done
  73.8 5.4 %multiply_reduce_fusion = f32[128,64]{1,0:T(8,128)} fusion(f32[128,64,128]{2,1,0:T(8,128)} %bitcast.30, pred[128,64]{1,0:T(8,128)(4,1)S(1)} %compare_and_fusion, bf16[128,64,128]{2,1,0:T(8,128)(2,1)} %all-to-all-done), kind=kLoop, calls=%fused_computation.5 | loop fusion | flops 4186112 | bytes 6332416 | tf_op jit(solution)/shard_map/reduce_sum | solution.py:50
  79.2 8.9 %all-to-all-start.2 = ((f32[128,1,64]{2,1,0:T(1,128)}), f32[128,1,64]{2,1,0:T(1,128)S(1)}, u32[]{:S(2)}, u32[]{:S(2)}) async-start(f32[128,1,64]{2,1,0:T(1,128)} %bitcast.6), calls=%async_computation.2 | async-start | bytes 131072 | tf_op jit(solution)/shard_map/all_to_all | solution.py:51
  88.2 9.4 %all-to-all-done.2 = f32[128,1,64]{2,1,0:T(1,128)S(1)} async-done(((f32[128,1,64]{2,1,0:T(1,128)}), f32[128,1,64]{2,1,0:T(1,128)S(1)}, u32[]{:S(2)}, u32[]{:S(2)}) %all-to-all-start.2) | async-done | bytes 32800 | tf_op jit(solution)/shard_map/all_to_all | solution.py:51
  98.0 0.8 reduce.11
  98.9 57.0 %scatter_fusion = f32[1024]{0:T(1024)S(1)} fusion(f32[1024]{0:T(1024)S(1)} %bitcast.29, s32[8192]{0:T(1024)S(1)} %bitcast.33, f32[8192]{0:T(1024)S(1)} %reshape.171), kind=kCustom, calls=%fused_computation.2 | custom fusion | flops 8192 | bytes 131072 | tf_op jit(solution)/shard_map/scatter-add | solution.py:53
  156.6 1.8 convert_reduce_fusion.1
  158.3 2.5 fusion.4
  160.8 1.0 convert_reduce_fusion
  161.9 2.6 convolution_bitcast_fusion
  164.5 32.9 %gather_fusion.1 = f32[8192]{0:T(1024)S(1)} fusion(f32[1024]{0:T(1024)S(1)} %get-tuple-element.41, s32[8192]{0:T(1024)S(1)} %broadcast_clamp_fusion), kind=kCustom, calls=%fused_computation.1 | custom fusion | bytes 98304 | tf_op jit(solution)/shard_map/jit(_take)/gather | solution.py:61
  198.1 4.6 %all-to-all-start.3 = ((f32[128,1,64]{2,1,0:T(1,128)}), f32[128,1,64]{2,1,0:T(1,128)S(1)}, u32[]{:S(2)}, u32[]{:S(2)}) async-start(f32[128,1,64]{2,1,0:T(1,128)} %bitcast.9), calls=%async_computation.3 | async-start | bytes 131072 | tf_op jit(solution)/shard_map/all_to_all | solution.py:62
  203.4 67.4 %all-reduce = (f32[512]{0:T(512)}, f32[256]{0:T(256)}, f32[256]{0:T(256)}) all-reduce(f32[512]{0:T(512)S(1)} %get-tuple-element.49, f32[256]{0:T(256)S(1)} %get-tuple-element.37, f32[256]{0:T(256)S(1)} %bitcast.36), channel_id=1, replica_groups=mesh['blk'=16,'rep'=8] {'blk','rep'}, use_global_device_ids=true, to_apply=%region_5.6 | all-reduce | flops 1024 | bytes 8192 | tf_op jit(solution)/shard_map/psum | solution.py:89
  270.9 0.8 reduce.12
  271.8 3.9 %bitcast_multiply_fusion = f32[8192,128]{1,0:T(8,128)} fusion(f32[8192]{0:T(1024)S(1)} %mul.66, bf16[128,64,128]{2,1,0:T(8,128)(2,1)} %all-to-all-done), kind=kLoop, calls=%fused_computation.4 | loop fusion | flops 2097152 | bytes 6324224 | tf_op jit(solution)/shard_map/mul | solution.py:65
  275.7 45.1 %scatter_custom_fusion.1 = f32[1024,128]{1,0:T(8,128)} fusion(s32[8192]{0:T(1024)S(1)} %bitcast.35, f32[8192,128]{1,0:T(8,128)} %bitcast_multiply_fusion, f32[]{:T(128)} %constant.32.clone.1), kind=kCustom, calls=%fused_computation.21 | custom fusion | flops 1048576 | bytes 524800 | tf_op jit(solution)/shard_map/scatter-add | solution.py:66
  320.7 2.7 multiply_subtract_fusion
  323.4 39.5 %all-reduce.4.cloned.1.call-done = (f32[1024,512]{0,1:T(8,128)}, f32[512,256]{1,0:T(8,128)}) async-done(((f32[1024,512]{0,1:T(8,128)}, f32[512,256]{1,0:T(8,128)}), (f32[1024,512]{0,1:T(8,128)}, f32[512,256]{1,0:T(8,128)})) %all-reduce.4.cloned.1.call-update) | async-done | bytes 2621456 | tf_op jit(solution)/shard_map/psum | solution.py:89
  362.9 2.9 copy.35
  365.8 0.8 copy.39
  (48 shorter events, 3.9 us)
Async XLA Ops:
  7.2 21.8 %copy-start = (bf16[1024,1024]{1,0:T(8,128)(2,1)S(1)}, bf16[1024,1024]{1,0:T(8,128)(2,1)}, u32[]{:S(2)}) copy-start(bf16[1024,1024]{1,0:T(8,128)(2,1)} %param.13) | copy-start | bytes 6291460
  8.8 24.6 %all-to-all-start.1 = ((s32[128,1,64]{2,1,0:T(1,128)}), s32[128,1,64]{2,1,0:T(1,128)S(1)}, u32[]{:S(2)}, u32[]{:S(2)}) async-start(s32[128,1,64]{2,1,0:T(1,128)} %bitcast.2), calls=%async_computation.1 | async-start | bytes 131072 | tf_op jit(solution)/shard_map/all_to_all | solution.py:44
  24.4 4.6 %copy-start.5 = (bf16[1024,512]{1,0:T(8,128)(2,1)S(1)}, bf16[1024,512]{1,0:T(8,128)(2,1)}, u32[]{:S(2)}) copy-start(bf16[1024,512]{1,0:T(8,128)(2,1)} %param.21) | copy-start | bytes 3145732
  24.4 4.5 %copy-start.8 = (f32[512]{0:T(512)S(1)}, f32[512]{0:T(512)}, u32[]{:S(2)}) copy-start(f32[512]{0:T(512)} %param.22) | copy-start | bytes 6148
  28.9 2.8 copy-start.6
  28.9 2.8 copy-start.9
  31.7 1.4 copy-start.11
  33.4 40.4 %all-to-all-start = ((bf16[128,64,128]{2,1,0:T(8,128)(2,1)}), bf16[128,64,128]{2,1,0:T(8,128)(2,1)}, u32[]{:S(2)}, u32[]{:S(2)}) async-start(bf16[128,64,128]{2,1,0:T(8,128)(2,1)} %broadcast_select_fusion), calls=%async_computation | async-start | bytes 4194304 | tf_op jit(solution)/shard_map/all_to_all | solution.py:43
  73.8 14.3 %copy-start.10 = (bf16[256]{0:T(256)(128)(2,1)S(1)}, bf16[256]{0:T(256)(128)(2,1)}, u32[]{:S(2)}) copy-start(bf16[256]{0:T(256)(128)(2,1)} %param.25) | copy-start | bytes 1540
  79.2 18.3 %all-to-all-start.2 = ((f32[128,1,64]{2,1,0:T(1,128)}), f32[128,1,64]{2,1,0:T(1,128)S(1)}, u32[]{:S(2)}, u32[]{:S(2)}) async-start(f32[128,1,64]{2,1,0:T(1,128)} %bitcast.6), calls=%async_computation.2 | async-start | bytes 131072 | tf_op jit(solution)/shard_map/all_to_all | solution.py:51
  98.9 57.0 %copy-start.4 = (s32[1024]{0:T(1024)S(1)}, s32[1024]{0:T(1024)}, u32[]{:S(2)}) copy-start(s32[1024]{0:T(1024)} %param.14) | copy-start | bytes 12292
  156.0 4.9 %copy-start.7 = (bf16[512,256]{1,0:T(8,128)(2,1)S(1)}, bf16[512,256]{1,0:T(8,128)(2,1)}, u32[]{:S(2)}) copy-start(bf16[512,256]{1,0:T(8,128)(2,1)} %param.23) | copy-start | bytes 786436
  156.0 4.9 %copy-start.12 = (f32[1024,512]{1,0:T(8,128)S(1)}, f32[1024,512]{1,0:T(8,128)}, u32[]{:S(2)}) copy-start(f32[1024,512]{1,0:T(8,128)} %get-tuple-element.46) | copy-start | bytes 6291460
  198.1 72.8 %all-to-all-start.3 = ((f32[128,1,64]{2,1,0:T(1,128)}), f32[128,1,64]{2,1,0:T(1,128)S(1)}, u32[]{:S(2)}, u32[]{:S(2)}) async-start(f32[128,1,64]{2,1,0:T(1,128)} %bitcast.9), calls=%async_computation.3 | async-start | bytes 131072 | tf_op jit(solution)/shard_map/all_to_all | solution.py:62
  202.7 160.2 %all-reduce.4.cloned.1.call-start = ((), (), s32[]{:S(2)}) async-start(), calls=%async_computation.4 | async-start | bytes 5242880 | tf_op jit(solution)/shard_map/psum | solution.py:89
  271.8 49.0 %copy-start.1 = (f32[1024,128]{1,0:T(8,128)S(1)}, f32[1024,128]{1,0:T(8,128)}, u32[]{:S(2)}) copy-start(f32[1024,128]{1,0:T(8,128)} %param.19) | copy-start | bytes 1572868
  271.8 49.0 %copy-start.2 = (f32[1024,128]{1,0:T(8,128)S(1)}, f32[1024,128]{1,0:T(8,128)}, u32[]{:S(2)}) copy-start(f32[1024,128]{1,0:T(8,128)} %param.20) | copy-start | bytes 1572868
  362.9 2.9 copy-start.3
Sparse Core Ops, SparseCore 0:
  209.1 153.7 all-reduce.3
where the time goes:
time: 374 us; the launch traced here: 373 us
  other arithmetic  127 us (34%)
  local copies, waits for them, and re-layouts  69 us (18%)
  blocking collectives  67.4 us (18%)
  waiting for transfers between devices  50.3 us (13%)
  starting transfers between devices  35.3 us (9%)
  between operations  14.3 us (4%)
  matrix products  10.7 us (3%)
    psum x1, blocking collectives, per_device(): lax.psum((grad_head, grad_w_two, grad_b_two, grad_w_one, grad_b_one), ('b...  67.4 us
    scatter-add x1, other arithmetic, per_device(): jnp.zeros((dense.shape[0],), jnp.float32).at[flat_example]  57 us
    scatter-add x1, other arithmetic, per_device(): grad_block = jnp.zeros_like(z_state).at[flat_block].add(contrib)  45.1 us
    psum x1, waiting for transfers between devices, per_device(): lax.psum((grad_head, grad_w_two, grad_b_two, grad_w_one, grad_b_one), ('b...  39.5 us
    gather x2, local copies, waits for them, and re-layouts, per_device(): tile_residual = jnp.take(residual, flat_example).reshape(owners, capacity)  32.9 us
    gather x1, local copies, waits for them, and re-layouts, per_device(): picked = jnp.take(weight, flat_block, axis=0)  27.8 us
    all_to_all x1, starting transfers between devices, per_device(): lax.all_to_all(tile_block, ('blk', 'rep'), split_axis=0, concat_axis=0, t...  11.5 us
    all_to_all x1, starting transfers between devices, per_device(): lax.all_to_all(masked, ('blk', 'rep'), split_axis=0, concat_axis=0, tiled...  10.2 us
  transfers between devices with their start and end apart: 5, of which 3 were waited for; matrix products, arithmetic and copies ran while one was open for 25% of the time, Pallas kernels for 0%

commit v1 on v0

--- a/solution.py
+++ b/solution.py
@@ -86,8 +86,11 @@
         dense, d_one, (((0,), (0,)), ((), ())), preferred_element_type=jnp.float32
     )
     grad_b_one = jnp.sum(d_one.astype(jnp.float32), axis=0)
-    grad_head, grad_w_two, grad_b_two, grad_w_one, grad_b_one = lax.psum(
-        (grad_head, grad_w_two, grad_b_two, grad_w_one, grad_b_one), ("blk", "rep")
+    follow_sources_all_for = lambda row_data: lax.psum(
+        lax.psum(row_data, axis_name="blk"), axis_name="rep"
+    )
+    grad_head, grad_w_two, grad_b_two, grad_w_one, grad_b_one = follow_sources_all_for(
+        (grad_head, grad_w_two, grad_b_two, grad_w_one, grad_b_one)
     )
     return (probability, z_new, n_new, grad_w_one, grad_b_one, grad_w_two, grad_b_two, grad_head)
 

time: 374 us -> 333 us (0.89)
  waiting for transfers between devices: 50.3 us -> 21.4 us
  blocking collectives: 67.4 us -> 54.7 us
    psum x1 -> x2, waiting for transfers between devices: 39.5 us -> 11.4 us  [the longest x1 11.4 us: per_device(): lax.psum(lax.psum(row_data, axis_name='blk'), axis_name='rep')]
    psum x1 -> x2, blocking collectives: 67.4 us -> 54.7 us  [the longest x1 34.2 us: per_device(): lax.psum(row_data, axis_name='blk')]
  transfers between devices with their start and end apart: 5 -> 6, of which waited for: 3 -> 3; matrix products, arithmetic and copies ran while one was open for 25% -> 38% of each run, Pallas kernels for 0% -> 0%
where the time goes in v1:
time: 333 us; the launch traced here: 331 us
  other arithmetic  125 us (38%)
  local copies, waits for them, and re-layouts  68.7 us (21%)
  blocking collectives  54.7 us (16%)
  starting transfers between devices  35.3 us (11%)
  waiting for transfers between devices  21.4 us (6%)
  between operations  14.3 us (4%)
  matrix products  10.9 us (3%)
    scatter-add x1, other arithmetic, per_device(): jnp.zeros((dense.shape[0],), jnp.float32).at[flat_example]  57 us
    scatter-add x1, other arithmetic, per_device(): grad_block = jnp.zeros_like(z_state).at[flat_block].add(contrib)  45.1 us
    psum x1, blocking collectives, per_device(): lax.psum(row_data, axis_name='blk')  34.2 us
    gather x2, local copies, waits for them, and re-layouts, per_device(): tile_residual = jnp.take(residual, flat_example).reshape(owners, capacity)  33 us
    gather x1, local copies, waits for them, and re-layouts, per_device(): picked = jnp.take(weight, flat_block, axis=0)  27.8 us
    psum x1, blocking collectives, per_device(): lax.psum(lax.psum(row_data, axis_name='blk'), axis_name='rep')  20.4 us
    all_to_all x1, starting transfers between devices, per_device(): lax.all_to_all(tile_block, ('blk', 'rep'), split_axis=0, concat_axis=0, t...  11.5 us
    psum x1, waiting for transfers between devices, per_device(): lax.psum(lax.psum(row_data, axis_name='blk'), axis_name='rep')  11.4 us
  transfers between devices with their start and end apart: 6, of which 3 were waited for; matrix products, arithmetic and copies ran while one was open for 38% of the time, Pallas kernels for 0%

profile of v1, /device:TPU:1, one launch (start us, length us, event | category | flops | bytes accessed | tf_op | source)
XLA Modules:
  0.0 330.7 jit_solution(10072336600690655035)
XLA Ops:
  7.2 1.6 copy.30
  8.8 11.5 %all-to-all-start.1 = ((s32[128,1,64]{2,1,0:T(1,128)}), s32[128,1,64]{2,1,0:T(1,128)S(1)}, u32[]{:S(2)}, u32[]{:S(2)}) async-start(s32[128,1,64]{2,1,0:T(1,128)} %bitcast.2), calls=%async_computation.1 | async-start | bytes 131072 | tf_op jit(solution)/shard_map/all_to_all | solution.py:44
  20.3 0.7 iota_compare_fusion
  21.1 0.8 copy.29
  22.1 4.5 %broadcast_select_fusion = bf16[128,64,128]{2,1,0:T(8,128)(2,1)} fusion(bf16[128,64,128]{2,1,0:T(8,128)(2,1)} %param.15, pred[128,64]{1,0:T(8,128)(4,1)S(1)} %iota_compare_fusion), kind=kLoop, calls=%fused_computation.10 | loop fusion | flops 1048576 | bytes 4202496 | tf_op jit(solution)/shard_map/jit(_where)/select_n | solution.py:41
  26.7 2.8 multiply_convert_fusion.1
  29.5 1.6 multiply_convert_fusion.3
  31.9 10.2 %all-to-all-start = ((bf16[128,64,128]{2,1,0:T(8,128)(2,1)}), bf16[128,64,128]{2,1,0:T(8,128)(2,1)}, u32[]{:S(2)}, u32[]{:S(2)}) async-start(bf16[128,64,128]{2,1,0:T(8,128)(2,1)} %broadcast_select_fusion), calls=%async_computation | async-start | bytes 4194304 | tf_op jit(solution)/shard_map/all_to_all | solution.py:43
  42.6 0.8 reduce.10
  43.6 27.8 %gather_fusion = f32[8192,128]{1,0:T(8,128)} fusion(f32[1024,128]{1,0:T(8,128)S(1)} %divide_select_fusion, s32[8192]{0:T(1024)S(1)} %broadcast_clamp_fusion.1), kind=kCustom, calls=%fused_computation | custom fusion | bytes 8421376 | tf_op jit(solution)/shard_map/jit(_take)/gather | solution.py:49
  71.4 0.9 all-to-all-done
  72.3 5.5 %multiply_reduce_fusion = f32[128,64]{1,0:T(8,128)} fusion(f32[128,64,128]{2,1,0:T(8,128)} %bitcast.30, pred[128,64]{1,0:T(8,128)(4,1)S(1)} %compare_and_fusion, bf16[128,64,128]{2,1,0:T(8,128)(2,1)} %all-to-all-done), kind=kLoop, calls=%fused_computation.5 | loop fusion | flops 4186112 | bytes 6332416 | tf_op jit(solution)/shard_map/reduce_sum | solution.py:50
  77.8 8.9 %all-to-all-start.2 = ((f32[128,1,64]{2,1,0:T(1,128)}), f32[128,1,64]{2,1,0:T(1,128)S(1)}, u32[]{:S(2)}, u32[]{:S(2)}) async-start(f32[128,1,64]{2,1,0:T(1,128)} %bitcast.6), calls=%async_computation.2 | async-start | bytes 131072 | tf_op jit(solution)/shard_map/all_to_all | solution.py:51
  87.0 9.1 %all-to-all-done.2 = f32[128,1,64]{2,1,0:T(1,128)S(1)} async-done(((f32[128,1,64]{2,1,0:T(1,128)}), f32[128,1,64]{2,1,0:T(1,128)S(1)}, u32[]{:S(2)}, u32[]{:S(2)}) %all-to-all-start.2) | async-done | bytes 32800 | tf_op jit(solution)/shard_map/all_to_all | solution.py:51
  96.6 0.8 reduce.11
  97.5 57.0 %scatter_fusion = f32[1024]{0:T(1024)S(1)} fusion(f32[1024]{0:T(1024)S(1)} %bitcast.29, s32[8192]{0:T(1024)S(1)} %bitcast.32, f32[8192]{0:T(1024)S(1)} %reshape.171), kind=kCustom, calls=%fused_computation.2 | custom fusion | flops 8192 | bytes 131072 | tf_op jit(solution)/shard_map/scatter-add | solution.py:53
  155.2 1.8 convert_reduce_fusion.1
  156.9 2.5 fusion.4
  159.4 1.0 convert_reduce_fusion
  160.4 2.6 convolution_bitcast_fusion
  163.1 32.9 %gather_fusion.1 = f32[8192]{0:T(1024)S(1)} fusion(f32[1024]{0:T(1024)S(1)} %get-tuple-element.46, s32[8192]{0:T(1024)S(1)} %broadcast_clamp_fusion), kind=kCustom, calls=%fused_computation.1 | custom fusion | bytes 98304 | tf_op jit(solution)/shard_map/jit(_take)/gather | solution.py:61
  196.1 0.6 and_select_fusion
  196.7 4.6 %all-to-all-start.3 = ((f32[128,1,64]{2,1,0:T(1,128)}), f32[128,1,64]{2,1,0:T(1,128)S(1)}, u32[]{:S(2)}, u32[]{:S(2)}) async-start(f32[128,1,64]{2,1,0:T(1,128)} %bitcast.9), calls=%async_computation.3 | async-start | bytes 131072 | tf_op jit(solution)/shard_map/all_to_all | solution.py:62
  201.6 34.2 %all-reduce = (f32[512]{0:T(512)S(1)}, f32[256]{0:T(256)S(1)}, f32[256]{0:T(256)S(1)}) all-reduce(f32[512]{0:T(512)S(1)} %get-tuple-element.54, f32[256]{0:T(256)S(1)} %get-tuple-element.42, f32[256]{0:T(256)S(1)} %bitcast.36), channel_id=1, replica_groups=mesh['blk'=16,'rep'=8] {'blk'}, use_global_device_ids=true, to_apply=%region_6.7 | all-reduce | flops 1024 | bytes 8192 | tf_op jit(solution)/shard_map/psum | solution.py:90
  235.8 20.4 %all-reduce.2 = (f32[512]{0:T(512)}, f32[256]{0:T(256)}, f32[256]{0:T(256)}) all-reduce(f32[512]{0:T(512)S(1)} %get-tuple-element.32, f32[256]{0:T(256)S(1)} %get-tuple-element.33, f32[256]{0:T(256)S(1)} %get-tuple-element.34), channel_id=1, replica_groups=mesh['blk'=16,'rep'=8] {'rep'}, use_global_device_ids=true, to_apply=%region_7.8 | all-reduce | flops 1024 | bytes 8192 | tf_op jit(solution)/shard_map/psum | solution.py:89
  256.2 0.8 reduce.12
  257.1 3.8 %bitcast_multiply_fusion = f32[8192,128]{1,0:T(8,128)} fusion(f32[8192]{0:T(1024)S(1)} %mul.66, bf16[128,64,128]{2,1,0:T(8,128)(2,1)} %all-to-all-done), kind=kLoop, calls=%fused_computation.4 | loop fusion | flops 2097152 | bytes 6324224 | tf_op jit(solution)/shard_map/mul | solution.py:65
  261.0 45.1 %scatter_custom_fusion.1 = f32[1024,128]{1,0:T(8,128)} fusion(s32[8192]{0:T(1024)S(1)} %bitcast.35, f32[8192,128]{1,0:T(8,128)} %bitcast_multiply_fusion, f32[]{:T(128)} %constant.32.clone.1), kind=kCustom, calls=%fused_computation.21 | custom fusion | flops 1048576 | bytes 524800 | tf_op jit(solution)/shard_map/scatter-add | solution.py:66
  306.1 2.7 multiply_subtract_fusion
  308.7 11.4 %all-reduce.9.cloned.1.call-done = (f32[1024,512]{0,1:T(8,128)}, f32[512,256]{1,0:T(8,128)}) async-done(((f32[1024,512]{0,1:T(8,128)}, f32[512,256]{1,0:T(8,128)}), (f32[1024,512]{0,1:T(8,128)}, f32[512,256]{1,0:T(8,128)})) %all-reduce.9.cloned.1.call-update) | async-done | bytes 2621456 | tf_op jit(solution)/shard_map/psum | solution.py:89
  320.1 2.9 copy.35
  323.1 0.8 copy.41
  (56 shorter events, 3.6 us)
Async XLA Ops:
  7.2 19.5 %copy-start = (bf16[1024,1024]{1,0:T(8,128)(2,1)S(1)}, bf16[1024,1024]{1,0:T(8,128)(2,1)}, u32[]{:S(2)}) copy-start(bf16[1024,1024]{1,0:T(8,128)(2,1)} %param.13) | copy-start | bytes 6291460
  8.8 23.1 %all-to-all-start.1 = ((s32[128,1,64]{2,1,0:T(1,128)}), s32[128,1,64]{2,1,0:T(1,128)S(1)}, u32[]{:S(2)}, u32[]{:S(2)}) async-start(s32[128,1,64]{2,1,0:T(1,128)} %bitcast.2), calls=%async_computation.1 | async-start | bytes 131072 | tf_op jit(solution)/shard_map/all_to_all | solution.py:44
  22.1 4.6 %copy-start.7 = (bf16[1024,512]{1,0:T(8,128)(2,1)S(1)}, bf16[1024,512]{1,0:T(8,128)(2,1)}, u32[]{:S(2)}) copy-start(bf16[1024,512]{1,0:T(8,128)(2,1)} %param.21) | copy-start | bytes 3145732
  22.1 4.6 %copy-start.10 = (f32[512]{0:T(512)S(1)}, f32[512]{0:T(512)}, u32[]{:S(2)}) copy-start(f32[512]{0:T(512)} %param.22) | copy-start | bytes 6148
  26.7 2.8 copy-start.8
  26.7 2.8 copy-start.11
  29.5 1.6 copy-start.13
  29.5 1.6 copy-start.1
  29.5 2.0 copy-start.2
  29.5 2.4 copy-start.12
  31.9 40.4 %all-to-all-start = ((bf16[128,64,128]{2,1,0:T(8,128)(2,1)}), bf16[128,64,128]{2,1,0:T(8,128)(2,1)}, u32[]{:S(2)}, u32[]{:S(2)}) async-start(bf16[128,64,128]{2,1,0:T(8,128)(2,1)} %broadcast_select_fusion), calls=%async_computation | async-start | bytes 4194304 | tf_op jit(solution)/shard_map/all_to_all | solution.py:43
  72.3 14.4 %copy-start.4 = (bf16[1024,256]{1,0:T(8,128)(2,1)S(1)}, bf16[1024,256]{1,0:T(8,128)(2,1)}, u32[]{:S(2)}) copy-start(bf16[1024,256]{1,0:T(8,128)(2,1)} %get-tuple-element.52) | copy-start | bytes 1572868
  77.8 18.3 %all-to-all-start.2 = ((f32[128,1,64]{2,1,0:T(1,128)}), f32[128,1,64]{2,1,0:T(1,128)S(1)}, u32[]{:S(2)}, u32[]{:S(2)}) async-start(f32[128,1,64]{2,1,0:T(1,128)} %bitcast.6), calls=%async_computation.2 | async-start | bytes 131072 | tf_op jit(solution)/shard_map/all_to_all | solution.py:51
  86.7 170.4 %all-reduce.7.cloned.1.call-start = ((), (), s32[]{:S(2)}) async-start(), calls=%async_computation.4 | async-start | bytes 5242880 | tf_op jit(solution)/shard_map/psum | solution.py:90
  97.5 57.0 %copy-start.6 = (s32[1024]{0:T(1024)S(1)}, s32[1024]{0:T(1024)}, u32[]{:S(2)}) copy-start(s32[1024]{0:T(1024)} %param.14) | copy-start | bytes 12292
  154.5 4.9 %copy-start.9 = (bf16[512,256]{1,0:T(8,128)(2,1)S(1)}, bf16[512,256]{1,0:T(8,128)(2,1)}, u32[]{:S(2)}) copy-start(bf16[512,256]{1,0:T(8,128)(2,1)} %param.23) | copy-start | bytes 786436
  154.5 4.9 %copy-start.14 = (f32[1024,512]{1,0:T(8,128)S(1)}, f32[1024,512]{1,0:T(8,128)}, u32[]{:S(2)}) copy-start(f32[1024,512]{1,0:T(8,128)} %get-tuple-element.51) | copy-start | bytes 6291460
  196.7 59.5 %all-to-all-start.3 = ((f32[128,1,64]{2,1,0:T(1,128)}), f32[128,1,64]{2,1,0:T(1,128)S(1)}, u32[]{:S(2)}, u32[]{:S(2)}) async-start(f32[128,1,64]{2,1,0:T(1,128)} %bitcast.9), calls=%async_computation.3 | async-start | bytes 131072 | tf_op jit(solution)/shard_map/all_to_all | solution.py:62
  201.3 118.8 %all-reduce.9.cloned.1.call-start = ((), (), s32[]{:S(2)}) async-start(), calls=%async_computation.5 | async-start | bytes 5242880 | tf_op jit(solution)/shard_map/psum | solution.py:89
  257.1 48.9 %copy-start.3 = (f32[1024,128]{1,0:T(8,128)S(1)}, f32[1024,128]{1,0:T(8,128)}, u32[]{:S(2)}) copy-start(f32[1024,128]{1,0:T(8,128)} %param.20) | copy-start | bytes 1572868
  320.1 2.9 copy-start.5
Sparse Core Ops, SparseCore 0:
  163.2 89.0 all-reduce.6
  257.3 62.8 all-reduce.8
